TPU v7x, 512 devices: a whole 4x4x16 slice. The times are simulated.
512 devices in a mesh: dp: 64 (over z, x), seq: 8 (over y, core).
Axes of the slice: x: 4, y: 4, z: 16, core: 2. Of those that a mesh axis runs over, the one named last changes fastest.
Arguments:
- acts: bfloat16 [65536, 4096], P('dp', 'seq'), may hold values from -6 to 6
- upstream: bfloat16 [65536, 1024], P(('dp', 'seq')), may hold values from -0.005859375 to 0.005859375
- keep_lists: int32 [64, 8], replicated, may hold values from 0 to 15, all different within a row
- left_gram: float32 [8, 64, 1, 64, 64], P('seq', 'dp'), as said below
- right_gram: float32 [8, 64, 1, 64, 64], P('seq', 'dp'), as said below
- left_basis: float32 [8, 64, 1, 64, 64], P('seq', 'dp'), may hold values from -0.75 to 0.75
- right_basis: float32 [8, 64, 1, 64, 64], P('seq', 'dp'), may hold values from -0.75 to 0.75
- second_moment: float32 [8, 64, 1, 64, 64], P('seq', 'dp'), may hold values from 0.004 to 0.04
Outputs:
- new_left: float32 [8, 64, 1, 64, 64], P('seq', 'dp')
- new_right: float32 [8, 64, 1, 64, 64], P('seq', 'dp')
- direction: float32 [8, 64, 1, 64, 64], P('seq', 'dp')
Inputs may be any that keep to these rules, and one draw needn't show every extreme that they name: `keep_lists`: each row lists 8 different column blocks, and every column block is kept in some row. `left_gram`: each block is symmetric. `right_gram`: each block is symmetric.
All inputs are finite; a program needn't handle non-finite values.
Results may differ from a plain program's by a relative error of at most 0.0003.
Values may be sent and summed in bfloat16 or wider, within the bound.
No kernel may reach another device: no remote copies, remote signals or barrier semaphores. Data moves between devices by JAX's collectives and lax.ppermute only.
A program may use at most 64 MiB of HBM per device.

v0:
```python
import jax
import jax.numpy as jnp
from jax import lax
from jax.sharding import PartitionSpec as P

BLOCK = 64


def precondition(gradient, left_gram, right_gram, left_basis, right_basis, second_moment):
    highest = lax.Precision.HIGHEST
    new_left = 0.95 * left_gram + 0.05 * jnp.einsum(
        "...ij,...kj->...ik", gradient, gradient, precision=highest
    )
    new_right = 0.95 * right_gram + 0.05 * jnp.einsum(
        "...ji,...jk->...ik", gradient, gradient, precision=highest
    )
    partial_rot = jnp.einsum("...ji,...jk->...ik", left_basis, gradient, precision=highest)
    rotated = jnp.einsum("...ij,...jk->...ik", partial_rot, right_basis, precision=highest)
    second = 0.95 * second_moment + 0.05 * rotated * rotated
    scaled = rotated / (jnp.sqrt(second) + 1e-08)
    partial_back = jnp.einsum("...ij,...jk->...ik", left_basis, scaled, precision=highest)
    direction = jnp.einsum("...ij,...kj->...ik", partial_back, right_basis, precision=highest)
    return (new_left, new_right, direction)


def per_device(
    acts, upstream, keep_lists, left_gram, right_gram, left_basis, right_basis, second_moment
):
    share_rows = acts.shape[1]
    share_blocks = share_rows // BLOCK
    kept_share = lax.dynamic_slice_in_dim(
        keep_lists, lax.axis_index("seq") * share_blocks, share_blocks, 0
    )
    gathered = lax.all_gather(upstream, "seq", axis=0, tiled=True)
    grad = lax.dot_general(
        acts, gathered, (((0,), (0,)), ((), ())), preferred_element_type=jnp.float32
    )
    tiles = grad.reshape(share_blocks, BLOCK, grad.shape[1] // BLOCK, BLOCK)
    picked = jnp.take_along_axis(tiles, kept_share[:, None, :, None], axis=2)
    packed = picked.transpose(0, 2, 1, 3)
    data_size = lax.axis_size("dp")
    outgoing = packed.reshape(data_size, -1, BLOCK * BLOCK)
    arrived = lax.all_to_all(outgoing, "dp", split_axis=0, concat_axis=0, tiled=True)
    owned_sum = jnp.sum(arrived, axis=0)
    gradient = owned_sum.reshape(1, 1, -1, BLOCK, BLOCK)
    new_left, new_right, direction = precondition(
        gradient, left_gram, right_gram, left_basis, right_basis, second_moment
    )
    return (new_left, new_right, direction)


def solution(mesh):
    in_specs = (
        P("dp", "seq"),
        P(("dp", "seq"), None),
        P(),
        P("seq", "dp", None, None, None),
        P("seq", "dp", None, None, None),
        P("seq", "dp", None, None, None),
        P("seq", "dp", None, None, None),
        P("seq", "dp", None, None, None),
    )
    out_specs = (
        P("seq", "dp", None, None, None),
        P("seq", "dp", None, None, None),
        P("seq", "dp", None, None, None),
    )
    return jax.shard_map(
        per_device, mesh=mesh, in_specs=in_specs, out_specs=out_specs, check_vma=False
    )
```

profile of v0, /device:TPU:2, one launch (start us, length us, event | category | flops | bytes accessed | tf_op | source)
XLA Modules:
  0.0 149.2 jit_solution(2693960995745928037)
XLA Ops:
  7.2 0.0 copy-start
  7.2 0.0 all-gather.2.cloned.1.call-start
  7.2 0.7 all-gather.2.cloned.1.call-update
  7.9 0.8 constant_dynamic-slice_fusion
  8.7 0.1 copy.17
  8.8 0.1 reshape.80
  8.9 38.8 %all-gather.2.cloned.1.call-done = bf16[1024,1024]{1,0:T(8,128)(2,1)} async-done(((bf16[128,1024]{1,0:T(8,128)(2,1)}), bf16[1024,1024]{1,0:T(8,128)(2,1)}) %all-gather.2.cloned.1.call-update) | async-done | bytes 2097168 | tf_op jit(solution)/shard_map/all_gather | solution.py:34
  47.6 2.9 %fusion.26 = f32[512,1024]{1,0:T(8,128)S(1)} fusion(bf16[1024,512]{1,0:T(8,128)(2,1)S(1)} %copy-done, bf16[1024,1024]{1,0:T(8,128)(2,1)} %all-gather.2.cloned.1.call-done), kind=kOutput, calls=%fused_computation.35 | convolution fusion | flops 1073741824 | bytes 5242880 | tf_op jit(solution)/shard_map/dot_general | solution.py:35
  50.5 2.6 %reshape.73 = f32[8,64,16,64]{3,2,1,0:T(8,128)} reshape(f32[512,1024]{1,0:T(8,128)S(1)} %fusion.26) | data formatting | bytes 4194304 | tf_op jit(solution)/shard_map/reshape | solution.py:38
  53.0 5.4 %copy.15 = f32[8,64,16,64]{3,1,2,0:T(8,128)} copy(f32[8,64,16,64]{3,2,1,0:T(8,128)} %reshape.73) | data formatting | bytes 4194304 | tf_op jit(solution)/shard_map/reshape | solution.py:38
  58.4 4.2 %gather_fusion = f32[64,64,64]{2,1,0:T(8,128)} fusion(f32[8,64,16,64]{3,1,2,0:T(8,128)} %copy.15, s32[64]{0:T(128)S(1)} %reshape.80), kind=kCustom, calls=%fused_computation | custom fusion | bytes 2097664 | tf_op jit(solution)/shard_map/jit(take_along_axis)/gather | solution.py:39
  62.6 1.8 %broadcast_select_fusion = f32[8,8,64,64]{3,2,1,0:T(8,128)S(1)} fusion(f32[8,8,64,64]{3,2,1,0:T(8,128)} %bitcast.57, pred[8,8]{1,0:T(8,128)(4,1)S(1)} %compare_and_fusion), kind=kLoop, calls=%fused_computation.8 | loop fusion | flops 262144 | bytes 2097216 | tf_op jit(solution)/shard_map/jit(take_along_axis)/select_n | solution.py:39
  64.4 2.3 %reshape.91 = f32[64,1,4096]{2,1,0:T(1,128)} reshape(f32[8,8,64,64]{3,2,1,0:T(8,128)S(1)} %broadcast_select_fusion) | data formatting | bytes 2097152 | tf_op jit(solution)/shard_map/reshape | solution.py:42
  66.7 0.0 copy-start.5
  66.7 71.4 %all_to_all.5 = f32[64,1,4096]{2,1,0:T(1,128)S(1)} all-to-all(f32[64,1,4096]{2,1,0:T(1,128)} %reshape.91), channel_id=1, replica_groups=mesh['dp'=64,'seq'=8] {'dp'}, dimensions={0} | all-to-all | bytes 2097152 | tf_op jit(solution)/shard_map/all_to_all | solution.py:43
  138.1 0.9 reduce_sum.9
  139.0 0.1 reshape.76
  139.1 0.8 fusion.2
  139.9 0.9 fusion.3
  140.7 0.2 fusion.17
  141.0 0.0 copy-done.1
  141.0 0.2 fusion.14
  141.2 0.3 fusion.10
  141.5 0.9 convolution_bitcast_fusion
  (11 shorter events, 0.0 us)
Async XLA Ops:
  7.2 40.5 %copy-start = (bf16[1024,512]{1,0:T(8,128)(2,1)S(1)}, bf16[1024,512]{1,0:T(8,128)(2,1)}, u32[]{:S(2)}) copy-start(bf16[1024,512]{1,0:T(8,128)(2,1)} %param.8) | copy-start | bytes 3145732
  7.2 40.4 %all-gather.2.cloned.1.call-start = ((), (), s32[]{:S(2)}) async-start(), calls=%async_computation.1 | async-start | bytes 2359296 | tf_op jit(solution)/shard_map/all_gather | solution.py:34
  66.7 72.4 %copy-start.3 = (f32[1,1,1,64,64]{4,3,2,1,0:T(8,128)S(1)}, f32[1,1,1,64,64]{4,3,2,1,0:T(8,128)}, u32[]{:S(2)}) copy-start(f32[1,1,1,64,64]{4,3,2,1,0:T(8,128)} %param.11) | copy-start | bytes 49156
  66.7 73.2 %copy-start.4 = (f32[1,1,1,64,64]{4,3,2,1,0:T(8,128)S(1)}, f32[1,1,1,64,64]{4,3,2,1,0:T(8,128)}, u32[]{:S(2)}) copy-start(f32[1,1,1,64,64]{4,3,2,1,0:T(8,128)} %param.12) | copy-start | bytes 49156
  66.7 74.0 %copy-start.2 = (f32[1,1,1,64,64]{4,3,2,1,0:T(8,128)S(1)}, f32[1,1,1,64,64]{4,3,2,1,0:T(8,128)}, u32[]{:S(2)}) copy-start(f32[1,1,1,64,64]{4,3,2,1,0:T(8,128)} %param.13) | copy-start | bytes 49156
  66.7 74.3 %copy-start.1 = (f32[1,1,1,64,64]{4,3,2,1,0:T(8,128)S(1)}, f32[1,1,1,64,64]{4,3,2,1,0:T(8,128)}, u32[]{:S(2)}) copy-start(f32[1,1,1,64,64]{4,3,2,1,0:T(8,128)} %param.14) | copy-start | bytes 49156
  66.7 74.5 %copy-start.5 = (f32[1,1,1,64,64]{4,3,2,1,0:T(8,128)S(1)}, f32[1,1,1,64,64]{4,3,2,1,0:T(8,128)}, u32[]{:S(2)}) copy-start(f32[1,1,1,64,64]{4,3,2,1,0:T(8,128)} %param.15) | copy-start | bytes 49156
Sparse Core Ops, SparseCore 0:
  10.1 37.4 all-gather.1
where the time goes:
time: 150 us; the launch traced here: 149 us
  blocking collectives  71.4 us (48%)
  waiting for transfers between devices  39.4 us (26%)
  local copies, waits for them, and re-layouts  15.4 us (10%)
  between operations  14.1 us (9%)
  matrix products  6.08 us (4%)
  other arithmetic  2.68 us (2%)
    all_to_all x1, blocking collectives, per_device(): lax.all_to_all(outgoing, 'dp', split_axis=0, concat_axis=0, tiled=True)  71.4 us
    all_gather x1, waiting for transfers between devices, per_device(): gathered = lax.all_gather(upstream, 'seq', axis=0, tiled=True)  38.8 us
    reshape x2, local copies, waits for them, and re-layouts, per_device(): tiles = grad.reshape(share_blocks, BLOCK, grad.shape[1] // BLOCK, BLOCK)  7.94 us
    gather x2, local copies, waits for them, and re-layouts, per_device(): picked = jnp.take_along_axis(tiles, kept_share[:, None, :, None], axis=2)  4.28 us
  transfers between devices with their start and end apart: 1, of which 1 were waited for; matrix products, arithmetic and copies ran while one was open for 1% of the time, Pallas kernels for 0%

commit v1 on v0

--- a/solution.py
+++ b/solution.py
@@ -4,6 +4,13 @@
 from jax.sharding import PartitionSpec as P
 
 BLOCK = 64
+
+
+def gather_over(shard, name, along):
+    size = lax.axis_size(name)
+    tiles = jnp.stack([shard for _ in range(size)])
+    tiles = lax.all_to_all(tiles, name, split_axis=0, concat_axis=0)
+    return jnp.concatenate(tiles, axis=along)
 
 
 def precondition(gradient, left_gram, right_gram, left_basis, right_basis, second_moment):
@@ -31,7 +38,7 @@
     kept_share = lax.dynamic_slice_in_dim(
         keep_lists, lax.axis_index("seq") * share_blocks, share_blocks, 0
     )
-    gathered = lax.all_gather(upstream, "seq", axis=0, tiled=True)
+    gathered = gather_over(upstream, "seq", 0)
     grad = lax.dot_general(
         acts, gathered, (((0,), (0,)), ((), ())), preferred_element_type=jnp.float32
     )

time: 150 us -> 130 us (0.87)
  waiting for transfers between devices: 39.4 us -> 25.6 us
  between operations: 14.1 us -> 0.77 us
  starting transfers between devices: 0.04 us -> 4.6 us
  blocking collectives: 71.4 us -> 73.4 us
    all_gather x1 -> x0, waiting for transfers between devices: 38.8 us -> none  [per_device(): gathered = lax.all_gather(upstream, 'seq', axis=0, tiled=True)]
    all_to_all x0 -> x1, waiting for transfers between devices: none -> 25.6 us  [gather_over(): tiles = lax.all_to_all(tiles, name, split_axis=0, concat_axis=0)]
    reshape x2 -> x0, local copies, waits for them, and re-layouts: 7.94 us -> none  [per_device(): tiles = grad.reshape(share_blocks, BLOCK, grad.shape[1] // BLOCK, BLOCK)]
    all_to_all x0 -> x1, starting transfers between devices: none -> 4.6 us  [gather_over(): tiles = lax.all_to_all(tiles, name, split_axis=0, concat_axis=0)]
    dot_general x0 -> x1, local copies, waits for them, and re-layouts: none -> 2.94 us  [per_device(): lax.dot_general(acts, gathered, (((0,), (0,)), ((), ())), preferred_eleme...]
    all_to_all x0 -> x1, local copies, waits for them, and re-layouts: none -> 2.59 us  [gather_over(): tiles = lax.all_to_all(tiles, name, split_axis=0, concat_axis=0)]
    unnamed x13 -> x19, local copies, waits for them, and re-layouts: 0.1 us -> 2.57 us
    all_to_all x1, blocking collectives: 71.4 us -> 73.4 us  [per_device(): lax.all_to_all(outgoing, 'dp', split_axis=0, concat_axis=0, tiled=True)]
where the time goes in v1:
time: 130 us
  blocking collectives  73.4 us (56%)
  waiting for transfers between devices  25.6 us (20%)
  local copies, waits for them, and re-layouts  15.5 us (12%)
  matrix products  7.17 us (6%)
  starting transfers between devices  4.6 us (4%)
  other arithmetic  2.68 us (2%)
    all_to_all x1, blocking collectives, per_device(): lax.all_to_all(outgoing, 'dp', split_axis=0, concat_axis=0, tiled=True)  73.4 us
    all_to_all x1, waiting for transfers between devices, gather_over(): tiles = lax.all_to_all(tiles, name, split_axis=0, concat_axis=0)  25.6 us
    all_to_all x1, starting transfers between devices, gather_over(): tiles = lax.all_to_all(tiles, name, split_axis=0, concat_axis=0)  4.6 us
    gather x2, local copies, waits for them, and re-layouts, per_device(): picked = jnp.take_along_axis(tiles, kept_share[:, None, :, None], axis=2)  4.3 us
    dot_general x1, matrix products, per_device(): lax.dot_general(acts, gathered, (((0,), (0,)), ((), ())), preferred_eleme...  3.94 us
    dot_general x1, local copies, waits for them, and re-layouts, per_device(): lax.dot_general(acts, gathered, (((0,), (0,)), ((), ())), preferred_eleme...  2.94 us
  transfers between devices with their start and end apart: 1, of which 1 were waited for; matrix products, arithmetic and copies ran while one was open for 1% of the time, Pallas kernels for 0%

profile of v1, /device:TPU:2, one launch (start us, length us, event | category | flops | bytes accessed | tf_op | source)
XLA Modules:
  0.0 129.7 jit_solution(8108660636090348208)
XLA Ops:
  0.6 0.0 copy-start
  0.6 1.1 copy.22
  1.8 1.6 %stack.2 = bf16[8,128,1024]{1,2,0:T(8,128)(2,1)} broadcast(bf16[128,1024]{0,1:T(8,128)(2,1)S(1)} %copy.22), dimensions={1,2} | broadcast | bytes 2359296 | tf_op jit(solution)/shard_map/stack | solution.py:11
  3.4 4.6 %all-to-all-start = ((bf16[8,128,1024]{1,2,0:T(8,128)(2,1)}), bf16[8,128,1024]{1,2,0:T(8,128)(2,1)S(1)}, u32[]{:S(2)}, u32[]{:S(2)}) async-start(bf16[8,128,1024]{1,2,0:T(8,128)(2,1)} %stack.2), calls=%async_computation | async-start | bytes 4194304 | tf_op jit(solution)/shard_map/all_to_all | solution.py:12
  8.0 1.3 %copy.21 = bf16[1024,512]{0,1:T(8,128)(2,1)} copy(bf16[1024,512]{1,0:T(8,128)(2,1)S(1)} %copy-done.1) | data formatting | bytes 2097152 | tf_op args[0]
  9.4 0.1 constant_dynamic-slice_fusion
  9.4 0.1 copy.26
  9.5 0.1 reshape.85
  9.6 25.6 %all-to-all-done = bf16[8,128,1024]{1,2,0:T(8,128)(2,1)S(1)} async-done(((bf16[8,128,1024]{1,2,0:T(8,128)(2,1)}), bf16[8,128,1024]{1,2,0:T(8,128)(2,1)S(1)}, u32[]{:S(2)}, u32[]{:S(2)}) %all-to-all-start) | async-done | bytes 2097184 | tf_op jit(solution)/shard_map/all_to_all | solution.py:12
  35.2 2.6 %copy.23 = bf16[8,128,1024]{2,1,0:T(8,128)(2,1)} copy(bf16[8,128,1024]{1,2,0:T(8,128)(2,1)S(1)} %all-to-all-done) | data formatting | bytes 4194304 | tf_op jit(solution)/shard_map/all_to_all | solution.py:12
  37.8 2.9 %copy.24 = bf16[1024,1024]{1,0:T(8,128)(2,1)S(1)} copy(bf16[1024,1024]{0,1:T(8,128)(2,1)} %bitcast.71) | data formatting | bytes 4194304 | tf_op jit(solution)/shard_map/dot_general | solution.py:42
  40.7 3.9 %fusion.26 = f32[8,64,16,64]{3,1,2,0:T(8,128)} fusion(bf16[8,64,1024,1]{2,1,3,0:T(8,128)(2,1)S(1)} %bitcast.73, bf16[16,64,1024,1]{2,1,0,3:T(8,128)(2,1)S(1)} %bitcast.72), kind=kOutput, calls=%fused_computation.35 | convolution fusion | flops 1073741824 | bytes 5242880 | tf_op jit(solution)/shard_map/dot_general | solution.py:42
  44.7 4.2 %gather_fusion = f32[64,64,64]{2,1,0:T(8,128)} fusion(f32[8,64,16,64]{3,1,2,0:T(8,128)} %fusion.26, s32[64]{0:T(128)S(1)} %reshape.85), kind=kCustom, calls=%fused_computation | custom fusion | bytes 2097664 | tf_op jit(solution)/shard_map/jit(take_along_axis)/gather | solution.py:46
  48.9 1.8 %broadcast_select_fusion = f32[8,8,64,64]{3,2,1,0:T(8,128)S(1)} fusion(f32[8,8,64,64]{3,2,1,0:T(8,128)} %bitcast.70, pred[8,8]{1,0:T(8,128)(4,1)S(1)} %compare_and_fusion), kind=kLoop, calls=%fused_computation.8 | loop fusion | flops 262144 | bytes 2097216 | tf_op jit(solution)/shard_map/jit(take_along_axis)/select_n | solution.py:46
  50.7 1.3 reshape.80
  52.0 73.4 %all_to_all.10 = f32[64,1,4096]{2,1,0:T(1,128)S(1)} all-to-all(f32[64,1,4096]{2,1,0:T(1,128)S(1)} %reshape.80), channel_id=1, replica_groups=mesh['dp'=64,'seq'=8] {'dp'}, dimensions={0} | all-to-all | bytes 2097152 | tf_op jit(solution)/shard_map/all_to_all | solution.py:50
  125.5 0.9 reduce_sum.9
  126.3 0.1 reshape.81
  126.4 0.8 fusion.2
  127.2 0.9 fusion.3
  128.1 0.2 fusion.17
  128.3 0.2 fusion.14
  128.6 0.3 fusion.10
  128.8 0.8 convolution_bitcast_fusion
  (17 shorter events, 0.1 us)
Async XLA Ops:
  0.6 127.5 %copy-start = (f32[1,1,1,64,64]{4,3,2,1,0:T(8,128)S(1)}, f32[1,1,1,64,64]{4,3,2,1,0:T(8,128)}, u32[]{:S(2)}) copy-start(f32[1,1,1,64,64]{4,3,2,1,0:T(8,128)} %param.13) | copy-start | bytes 49156
  3.4 4.6 %copy-start.1 = (bf16[1024,512]{1,0:T(8,128)(2,1)S(1)}, bf16[1024,512]{1,0:T(8,128)(2,1)}, u32[]{:S(2)}) copy-start(bf16[1024,512]{1,0:T(8,128)(2,1)} %param.8) | copy-start | bytes 3145732
  3.4 31.8 %all-to-all-start = ((bf16[8,128,1024]{1,2,0:T(8,128)(2,1)}), bf16[8,128,1024]{1,2,0:T(8,128)(2,1)S(1)}, u32[]{:S(2)}, u32[]{:S(2)}) async-start(bf16[8,128,1024]{1,2,0:T(8,128)(2,1)} %stack.2), calls=%async_computation | async-start | bytes 4194304 | tf_op jit(solution)/shard_map/all_to_all | solution.py:12
  8.0 1.3 %copy-start.6 = (s32[64,8]{0,1:T(8,128)S(1)}, s32[64,8]{0,1:T(8,128)}, u32[]{:S(2)}) copy-start(s32[64,8]{0,1:T(8,128)} %param.10) | copy-start | bytes 6148
  37.8 3.0 %copy-start.2 = (bf16[1024,512]{0,1:T(8,128)(2,1)S(1)}, bf16[1024,512]{0,1:T(8,128)(2,1)}, u32[]{:S(2)}) copy-start(bf16[1024,512]{0,1:T(8,128)(2,1)} %copy.21) | copy-start | bytes 3145732
  52.0 74.4 %copy-start.4 = (f32[1,1,1,64,64]{4,3,2,1,0:T(8,128)S(1)}, f32[1,1,1,64,64]{4,3,2,1,0:T(8,128)}, u32[]{:S(2)}) copy-start(f32[1,1,1,64,64]{4,3,2,1,0:T(8,128)} %param.11) | copy-start | bytes 49156
  52.0 75.2 %copy-start.5 = (f32[1,1,1,64,64]{4,3,2,1,0:T(8,128)S(1)}, f32[1,1,1,64,64]{4,3,2,1,0:T(8,128)}, u32[]{:S(2)}) copy-start(f32[1,1,1,64,64]{4,3,2,1,0:T(8,128)} %param.12) | copy-start | bytes 49156
  52.0 76.3 %copy-start.3 = (f32[1,1,1,64,64]{4,3,2,1,0:T(8,128)S(1)}, f32[1,1,1,64,64]{4,3,2,1,0:T(8,128)}, u32[]{:S(2)}) copy-start(f32[1,1,1,64,64]{4,3,2,1,0:T(8,128)} %param.14) | copy-start | bytes 49156
  52.0 76.6 %copy-start.7 = (f32[1,1,1,64,64]{4,3,2,1,0:T(8,128)S(1)}, f32[1,1,1,64,64]{4,3,2,1,0:T(8,128)}, u32[]{:S(2)}) copy-start(f32[1,1,1,64,64]{4,3,2,1,0:T(8,128)} %param.15) | copy-start | bytes 49156
